TPU v7x, 256 devices: a whole 4x4x8 slice. The times are simulated.
256 devices in a mesh: section: 16 (over z_lo, y, core), dp: 16 (over z_hi, x).
Axes of the slice: x: 4, y: 4, z: 8 (z_hi: 4, z_lo: 2; z = z_hi * 2 + z_lo), core: 2. Of those that a mesh axis runs over, the one named last changes fastest.
Arguments:
- w_in: bfloat16 [16, 5120, 4096], P('section', 'dp'), may hold values from -0.09375 to 0.09375
- w_out: bfloat16 [16, 5120, 4096], P('section', 'dp'), may hold values from -0.078125 to 0.078125
- input_stash: bfloat16 [16, 2, 128, 4096], P('section', None, 'dp'), may hold values from -6 to 6
- hidden_stash: bfloat16 [16, 2, 128, 5120], P('section', None, None, 'dp'), may hold values from -6 to 6
- gate_stash: float32 [16, 2, 128], P('section'), may hold values from 0.25 to 1
- block_pick: int32 [16, 2], P('section'), may hold values from 0 to 1
- slot_order: int32 [16, 2], P('section'), may hold values from 0 to 1, each once within a row
- arriving: bfloat16 [16, 2, 128, 4096], P('section', None, 'dp'), may hold values from -6 to 6
- loss_grads: bfloat16 [1, 2, 128, 4096], P(None, None, 'dp'), may hold values from -6 to 6
Outputs:
- passed: bfloat16 [16, 2, 2, 128, 4096], P('section', None, None, 'dp')
- grad_in: bfloat16 [16, 5120, 4096], P('section', 'dp')
- grad_out: bfloat16 [16, 5120, 4096], P('section', 'dp')
- gate_grads: float32 [16, 2, 128], P('section')
Inputs may be any that keep to these rules, and one draw needn't show every extreme that they name: Each row of slot_order holds every slot 0 to 1 once.
All inputs are finite; a program needn't handle non-finite values.
Results may differ from a plain program's by a relative error of at most 0.0055.
Values may be sent and summed in bfloat16 or wider, within the bound.
A program may use at most 128 MiB of HBM per device.

v0:
```python
import jax
import jax.numpy as jnp
from jax import lax
from jax.sharding import PartitionSpec as P


def shifted_2(block, axis, distance):
    devices = range(lax.axis_size(axis))
    route = [(i - distance, i) for i in devices if i - distance in devices]
    return lax.ppermute(block, axis, route)


def per_device(
    w_in, w_out, input_stash, hidden_stash, gate_stash, block_pick, slot_order, arriving, loss_grads
):
    in_weight = w_in[0]
    out_weight = w_out[0]
    ticks = slot_order.shape[1]
    blocks = arriving.shape[1]
    is_top = lax.axis_index("section") == lax.axis_size("section") - 1
    contract = (((0,), (0,)), ((), ()))

    def section_tick(incoming, tick_index):
        slot_id = slot_order[0, tick_index]
        block_id = block_pick[0, slot_id]
        gate_vals = gate_stash[0, slot_id]
        pre_act = hidden_stash[0, slot_id]
        own_rows = incoming[block_id]
        rows_input, rows_grad = (
            lax.all_gather(input_stash[0, slot_id], "dp", axis=0, tiled=True),
            lax.all_gather(own_rows, "dp", axis=0, tiled=True),
        )
        upstream = lax.dot_general(
            rows_grad, out_weight, (((1,), (1,)), ((), ())), preferred_element_type=jnp.float32
        )
        active = jnp.maximum(pre_act.astype(jnp.float32), 0.0)
        hid_grad = jnp.where(pre_act > 0, upstream * gate_vals[:, None], 0.0).astype(jnp.bfloat16)
        input_part = lax.psum_scatter(
            jnp.dot(hid_grad, in_weight, preferred_element_type=jnp.float32),
            "dp",
            scatter_dimension=0,
            tiled=True,
        )
        placed = jnp.where((jnp.arange(blocks) == block_id)[:, None, None], input_part[None], 0.0)
        updated = (incoming.astype(jnp.float32) + placed).astype(jnp.bfloat16)
        gate_part = jnp.sum(active * upstream, axis=1)
        gate_part = lax.psum(gate_part, "dp")
        weighted = (active * gate_vals[:, None]).astype(jnp.bfloat16)
        return (updated, gate_part, (rows_grad, weighted, hid_grad, rows_input))

    def weight_terms(pieces):
        rows_grad, weighted, hid_grad, rows_input = pieces
        out_term = lax.dot_general(
            weighted, rows_grad, contract, preferred_element_type=jnp.float32
        )
        in_term = lax.dot_general(
            hid_grad, rows_input, contract, preferred_element_type=jnp.float32
        )
        return (out_term, in_term)

    start_sums = (jnp.zeros(out_weight.shape, jnp.float32), jnp.zeros(in_weight.shape, jnp.float32))

    def advance(carry, extra):
        incoming, sums = carry
        tick_index, loss_rows = extra
        updated, gate_part, pieces = section_tick(incoming, tick_index)
        terms = weight_terms(pieces)
        sums = (sums[0] + terms[0], sums[1] + terms[1])
        shifted = shifted_2(updated, "section", -1)
        following = jnp.where(is_top, loss_rows, shifted)
        return ((following, sums), (updated, gate_part))

    (last_in, sums), (early_out, early_gate) = lax.scan(
        advance, (arriving[0], start_sums), (jnp.arange(ticks - 1), loss_grads)
    )
    last_out, last_gate, last_pieces = section_tick(last_in, ticks - 1)
    terms = weight_terms(last_pieces)
    out_sum = sums[0] + terms[0]
    in_sum = sums[1] + terms[1]
    passed = jnp.concatenate([early_out, last_out[None]], axis=0)
    gate_parts = jnp.concatenate([early_gate, last_gate[None]], axis=0)
    onehot = (slot_order[0][:, None] == jnp.arange(ticks)[None, :]).astype(jnp.float32)
    gate_grads = jnp.einsum("tp,tr->pr", onehot, gate_parts, precision=lax.Precision.HIGHEST)
    return (
        passed[None],
        in_sum.astype(jnp.bfloat16)[None],
        out_sum.astype(jnp.bfloat16)[None],
        gate_grads[None],
    )


def solution(mesh):
    placed = (
        P("section", "dp", None),
        P("section", "dp", None),
        P("section", None, "dp", None),
        P("section", None, None, "dp"),
        P("section", None, None),
        P("section", None),
        P("section", None),
        P("section", None, "dp", None),
        P(None, None, "dp", None),
    )
    return jax.shard_map(
        per_device,
        mesh=mesh,
        in_specs=placed,
        out_specs=(
            P("section", None, None, "dp", None),
            P("section", "dp", None),
            P("section", "dp", None),
            P("section", None, None),
        ),
        check_vma=False,
    )
```

profile of v0, /device:TPU:8, one launch (start us, length us, event | category | flops | bytes accessed | tf_op | source)
XLA Modules:
  0.0 431.0 jit_solution(4442010572938618943)
XLA Ops:
  7.2 0.0 copy-start
  7.2 0.0 all-gather.9.cloned.1.call-start
  7.2 1.4 fusion.47
  12.5 1.3 constant_dynamic-slice_fusion.4
  15.8 1.5 constant_dynamic-slice_fusion.6
  17.3 0.0 all-gather.9.cloned.1.call-update
  17.3 0.0 reduce-scatter.3.cloned.1.call-start
  17.3 0.8 fusion.42
  18.1 56.0 %all-gather.9.cloned.1.call-done = bf16[1,1,128,4096]{3,2,1,0:T(8,128)(2,1)} async-done(((bf16[1,1,8,4096]{3,2,1,0:T(8,128)(2,1)}), bf16[1,1,128,4096]{3,2,1,0:T(8,128)(2,1)}) %all-gather.9.cloned.1.call-update) | async-done | bytes 1048592 | tf_op jit(solution)/shard_map/while/body/eval_jaxpr/all_gather | solution.py:31
  74.1 2.9 select_convert_fusion.1
  76.9 0.0 copy-start.2
  77.0 0.0 copy-start.4
  77.0 2.1 fusion.6
  79.0 0.0 reduce-scatter.3.cloned.1.call-update
  79.1 0.0 all-gather.11.cloned.1.call-start
  79.1 0.7 iota_compare_fusion.1
  79.8 85.0 %reduce-scatter.3.cloned.1.call-done = f32[8,4096]{1,0:T(8,128)} async-done(((f32[128,4096]{1,0:T(8,128)}), f32[8,4096]{1,0:T(8,128)}) %reduce-scatter.3.cloned.1.call-update) | async-done | bytes 131088 | tf_op jit(solution)/shard_map/while/body/eval_jaxpr/reduce_scatter | solution.py:38
  164.7 0.0 copy-done.2
  164.7 1.0 fusion.22
  165.7 1.9 collective-permute-start
  169.6 0.6 collective-permute-done
  170.2 0.0 copy-done.4
  170.2 0.9 bitcast_select_fusion
  171.1 0.6 constant_dynamic-slice_fusion.3
  171.7 0.0 all-gather.11.cloned.1.call-update
  171.8 0.0 all-gather.13.cloned.1.call-start
  171.8 1.5 constant_dynamic-slice_fusion
  173.4 0.0 all-gather.13.cloned.1.call-update
  173.4 0.0 all-gather.15.cloned.1.call-start
  173.4 0.5 all-gather.15.cloned.1.call-update
  174.0 0.0 reduce-scatter.5.cloned.1.call-start
  174.0 51.0 %all-gather.11.cloned.1.call-done = bf16[1,128,4096]{2,1,0:T(8,128)(2,1)} async-done(((bf16[1,8,4096]{2,1,0:T(8,128)(2,1)}), bf16[1,128,4096]{2,1,0:T(8,128)(2,1)}) %all-gather.11.cloned.1.call-update) | async-done | bytes 1048592 | tf_op jit(solution)/shard_map/all_gather | solution.py:31
  225.0 2.9 fusion.26
  227.9 2.1 fusion.4
  230.0 0.0 reduce-scatter.5.cloned.1.call-update
  230.0 0.7 iota_compare_fusion
  230.7 4.4 %fusion.17 = f32[320,4096]{1,0:T(8,128)} fusion(bf16[1,1,128,4096]{3,2,1,0:T(8,128)(2,1)} %all-gather.9.cloned.1.call-done, f32[128]{0:T(128)S(1)} %get-tuple-element.42, bf16[1,2,128,320]{2,3,1,0:T(8,128)(2,1)S(1)} %copy-done.1, s32[]{:T(128)S(6)} %select_n.57), kind=kOutput, calls=%fused_computation.20 | convolution fusion | flops 335708160 | bytes 6373892 | tf_op jit(solution)/shard_map/while/body/eval_jaxpr/dot_general | solution.py:53
  235.1 43.8 %all-gather.13.cloned.1.call-done = bf16[1,1,128,4096]{3,2,1,0:T(8,128)(2,1)} async-done(((bf16[1,1,8,4096]{3,2,1,0:T(8,128)(2,1)}), bf16[1,1,128,4096]{3,2,1,0:T(8,128)(2,1)}) %all-gather.13.cloned.1.call-update) | async-done | bytes 1048592 | tf_op jit(solution)/shard_map/while/body/eval_jaxpr/all_gather | solution.py:30
  278.9 4.4 %fusion.13 = f32[320,4096]{1,0:T(8,128)} fusion(bf16[128,320]{0,1:T(8,128)(2,1)S(1)} %get-tuple-element.62, bf16[1,1,128,4096]{3,2,1,0:T(8,128)(2,1)} %all-gather.13.cloned.1.call-done), kind=kOutput, calls=%fused_computation.16 | convolution fusion | flops 335544320 | bytes 6373376 | tf_op jit(solution)/shard_map/while/body/eval_jaxpr/dot_general | solution.py:56
  283.3 0.1 fusion.20
  283.4 42.8 %all-reduce = (f32[1,128]{1,0:T(1,128)S(1)}, f32[1,128]{1,0:T(1,128)S(1)}) all-reduce(f32[1,128]{1,0:T(1,128)S(1)} %bitcast.89, f32[1,128]{1,0:T(1,128)S(1)} %bitcast.88), channel_id=1, replica_groups=mesh['section'=16,'dp'=16] {'dp'}, use_global_device_ids=true, to_apply=%region_5.6 | all-reduce | flops 256 | bytes 2048 | tf_op jit(solution)/shard_map/psum | solution.py:47
  326.2 0.8 convolution_bitcast_fusion
  327.0 5.2 %fusion.2 = bf16[1,320,4096]{2,1,0:T(8,128)(2,1)} fusion(f32[320,4096]{1,0:T(8,128)} %fusion.17, bf16[1,128,4096]{2,1,0:T(8,128)(2,1)} %all-gather.11.cloned.1.call-done, f32[128]{0:T(128)S(1)} %get-tuple-element.41, bf16[1,2,128,320]{2,3,1,0:T(8,128)(2,1)S(1)} %copy-done.1, s32[]{:T(128)S(6)} %select_n.64), kind=kOutput, calls=%fused_computation.4 | convolution fusion | flops 338329600 | bytes 8995332 | tf_op jit(solution)/shard_map/dot_general | solution.py:53
  332.1 0.2 all-gather.15.cloned.1.call-done
  332.3 5.1 %fusion.3 = bf16[1,320,4096]{2,1,0:T(8,128)(2,1)} fusion(f32[320,4096]{1,0:T(8,128)} %fusion.13, bf16[128,320]{0,1:T(8,128)(2,1)S(1)} %get-tuple-element.38, bf16[1,1,128,4096]{3,2,1,0:T(8,128)(2,1)} %all-gather.15.cloned.1.call-done), kind=kOutput, calls=%fused_computation.5 | convolution fusion | flops 338165760 | bytes 8994816 | tf_op jit(solution)/shard_map/dot_general | solution.py:56
  337.4 84.9 %reduce-scatter.5.cloned.1.call-done = f32[8,4096]{1,0:T(8,128)} async-done(((f32[128,4096]{1,0:T(8,128)}), f32[8,4096]{1,0:T(8,128)}) %reduce-scatter.5.cloned.1.call-update) | async-done | bytes 131088 | tf_op jit(solution)/shard_map/reduce_scatter | solution.py:38
  422.4 1.0 fusion.27
  423.4 0.7 maximum_bitcast_fusion
  (7 shorter events, 0.0 us)
Async XLA Ops:
  7.2 69.8 %copy-start = (bf16[1,320,4096]{2,1,0:T(8,128)(2,1)S(1)}, bf16[1,320,4096]{2,1,0:T(8,128)(2,1)}, u32[]{:S(2)}) copy-start(bf16[1,320,4096]{2,1,0:T(8,128)(2,1)} %param.9) | copy-start | bytes 7864324
  7.2 66.9 %all-gather.9.cloned.1.call-start = ((), (), s32[]{:S(2)}) async-start(), calls=%async_computation.4 | async-start | bytes 1114112 | tf_op jit(solution)/shard_map/while/body/eval_jaxpr/all_gather | solution.py:31
  17.3 147.5 %reduce-scatter.3.cloned.1.call-start = ((), (), s32[]{:S(2)}) async-start(), calls=%async_computation.2 | async-start | bytes 2228224 | tf_op jit(solution)/shard_map/while/body/eval_jaxpr/reduce_scatter | solution.py:38
  76.9 87.8 %copy-start.2 = (bf16[1,2,8,4096]{3,2,1,0:T(8,128)(2,1)S(1)}, bf16[1,2,8,4096]{3,2,1,0:T(8,128)(2,1)}, u32[]{:S(2)}) copy-start(bf16[1,2,8,4096]{3,2,1,0:T(8,128)(2,1)} %param.16) | copy-start | bytes 393220
  77.0 93.2 %copy-start.4 = (bf16[1,2,8,4096]{3,2,1,0:T(8,128)(2,1)S(1)}, bf16[1,2,8,4096]{3,2,1,0:T(8,128)(2,1)}, u32[]{:S(2)}) copy-start(bf16[1,2,8,4096]{3,2,1,0:T(8,128)(2,1)} %param.17) | copy-start | bytes 393220
  79.0 145.9 %copy-start.1 = (bf16[1,2,128,320]{2,3,1,0:T(8,128)(2,1)S(1)}, bf16[1,2,128,320]{2,3,1,0:T(8,128)(2,1)}, u32[]{:S(2)}) copy-start(bf16[1,2,128,320]{2,3,1,0:T(8,128)(2,1)} %param.12) | copy-start | bytes 491524
  79.1 145.9 %all-gather.11.cloned.1.call-start = ((), (), s32[]{:S(2)}) async-start(), calls=%async_computation.5 | async-start | bytes 1114112 | tf_op jit(solution)/shard_map/all_gather | solution.py:31
  165.7 4.4 %collective-permute-start = (bf16[2,8,4096]{2,1,0:T(8,128)(2,1)S(1)}, bf16[2,8,4096]{2,1,0:T(8,128)(2,1)}, u32[]{:S(2)}, u32[]{:S(2)}) collective-permute-start(bf16[2,8,4096]{2,1,0:T(8,128)(2,1)S(1)} %fusion.22), channel_id=1, source_target_pairs={{16,0},{32,16},{48,32},{64,48},{80,64},{96,80},{112,96},{128,112},... | collective-permute-start | bytes 393224 | tf_op jit(solution)/shard_map/while/body/eval_jaxpr/ppermute | solution.py:10
  171.8 107.1 %all-gather.13.cloned.1.call-start = ((), (), s32[]{:S(2)}) async-start(), calls=%async_computation.6 | async-start | bytes 1114112 | tf_op jit(solution)/shard_map/while/body/eval_jaxpr/all_gather | solution.py:30
  173.4 158.9 %all-gather.15.cloned.1.call-start = ((), (), s32[]{:S(2)}) async-start(), calls=%async_computation.7 | async-start | bytes 1114112 | tf_op jit(solution)/shard_map/all_gather | solution.py:30
  174.0 248.4 %reduce-scatter.5.cloned.1.call-start = ((), (), s32[]{:S(2)}) async-start(), calls=%async_computation.3 | async-start | bytes 2228224 | tf_op jit(solution)/shard_map/reduce_scatter | solution.py:38
  235.1 48.2 %copy-start.3 = (f32[8,4096]{1,0:T(8,128)S(1)}, f32[8,4096]{1,0:T(8,128)}, u32[]{:S(2)}) copy-start(f32[8,4096]{1,0:T(8,128)} %reduce-scatter.3.cloned.1.call-done) | copy-start | bytes 393220
  235.1 91.1 %copy-start.5 = (s32[1,2]{1,0:T(1,128)S(1)}, s32[1,2]{1,0:T(1,128)}, u32[]{:S(2)}) copy-start(s32[1,2]{1,0:T(1,128)} %param.15) | copy-start | bytes 28
Sparse Core Ops, SparseCore 0:
  17.4 56.6 all-gather.8
  79.2 85.5 reduce-scatter.2
  171.9 53.0 all-gather.10
  228.1 50.7 all-gather.12
  282.1 50.1 all-gather.14
  336.1 86.1 reduce-scatter.4
where the time goes:
time: 432 us; the launch traced here: 431 us
  waiting for transfers between devices  322 us (75%)
  blocking collectives  42.8 us (10%)
  matrix products  29.8 us (7%)
  between operations  22 us (5%)
  local copies, waits for them, and re-layouts  7.18 us (2%)
  other arithmetic  5.06 us (1%)
    reduce_scatter x2, waiting for transfers between devices, section_tick(): lax.psum_scatter(jnp.dot(hid_grad, in_weight, preferred_element_type=jnp....  170 us
    all_gather x2, waiting for transfers between devices, section_tick(): lax.all_gather(own_rows, 'dp', axis=0, tiled=True)  107 us
    all_gather x2, waiting for transfers between devices, section_tick(): lax.all_gather(input_stash[0, slot_id], 'dp', axis=0, tiled=True)  44 us
    psum x1, blocking collectives, section_tick(): gate_part = lax.psum(gate_part, 'dp')  42.8 us
    dot_general x2, matrix products, weight_terms(): lax.dot_general(weighted, rows_grad, contract, preferred_element_type=jnp...  9.57 us
    dot_general x2, matrix products, weight_terms(): lax.dot_general(hid_grad, rows_input, contract, preferred_element_type=jn...  9.5 us
  transfers between devices with their start and end apart: 7, of which 7 were waited for; matrix products, arithmetic and copies ran while one was open for 7% of the time, Pallas kernels for 0%

commit v1 on v0

v1 whole, which is shorter than its diff:
```python
import functools

import jax
import jax.numpy as jnp
from jax import lax
from jax.experimental import pallas as pl
from jax.experimental.pallas import tpu as pltpu
from jax.sharding import PartitionSpec as P

MESH = pl.DeviceIdType.MESH
SIDE = 4
CHUNKS = 4
GATHER_ORDER = ("z", "z", "z", "x")
SCATTER_ORDER = ("x", "x", "x", "z")
BF16 = jnp.bfloat16
F32 = jnp.float32


def kernel(
    w_in, w_out, stash, hidden, gates, pick, order, arriving, loss,
    passed, grad_in, grad_out, gate_grads,
    win, wout, rows, saved, part, recv1, mid, recv2, inc, up, hid_t, wgt_t, hid, pre_t, gpart, gate_z, gate_x, out_in, out_out,
    ag_send, ag_recv, rs_send, rs_recv, pm_send, pm_recv, gt_send, gt_recv, local,
):
    ticks, width = 2, w_in.shape[2]
    cols_of = width // CHUNKS
    s, d = lax.axis_index("section"), lax.axis_index("dp")
    a, b = d // SIDE, d % SIDE
    sections = lax.axis_size("section")
    below, above = lax.rem(s + sections - 1, sections), lax.rem(s + 1, sections)

    def spot(axis, k):
        return ((a + k) % SIDE if axis == "z" else a, (b + k) % SIDE if axis == "x" else b)

    def peer(axis, k):
        pa, pb = spot(axis, k)
        return (s, pa * SIDE + pb)

    def cols(c):
        return pl.ds(c * cols_of, cols_of)

    barrier = pltpu.get_barrier_semaphore()
    for axis in ("z", "x"):
        for k in (1, 2, 3):
            pl.semaphore_signal(barrier, inc=1, device_id=peer(axis, k), device_id_type=MESH)
    for other in (below, above):
        pl.semaphore_signal(barrier, inc=1, device_id=(other, d), device_id_type=MESH)

    load_out = pltpu.make_async_copy(w_out.at[0], wout, local.at[0])
    load_in = pltpu.make_async_copy(w_in.at[0], win, local.at[1])
    load_out.start()
    load_in.start()

    slots = [order[0, t] for t in range(ticks)]
    blocks = [pick[0, slots[t]] for t in range(ticks)]
    rows[0, a, b] = arriving[0, blocks[0]]
    for t in range(ticks):
        saved[t, a, b] = stash[0, slots[t]]

    pl.semaphore_wait(barrier, 8)

    gpart[...] = jnp.zeros_like(gpart)
    sent = []

    def remote(src, dst, send_sem, recv_sem, device):
        return pltpu.make_async_remote_copy(
            src_ref=src, dst_ref=dst, send_sem=send_sem, recv_sem=recv_sem, device_id=device, device_id_type=MESH
        )

    def gather_copy(buf, which, c, stage, k):
        first = GATHER_ORDER[c]
        if stage == 0:
            axis = first
            view = buf.at[a, b, :, cols(c)]
        elif first == "z":
            axis = "x"
            view = buf.at[:, b, :, cols(c)]
        else:
            axis = "z"
            view = buf.at[a, :, :, cols(c)]
        return remote(
            view, view, ag_send.at[which, c, stage, k - 1], ag_recv.at[which, c, stage, k - 1], peer(axis, k)
        )

    def gather_start(buf, which, c, stage):
        for k in (1, 2, 3):
            copy = gather_copy(buf, which, c, stage, k)
            copy.start()
            sent.append(copy)

    def gather_wait(buf, which, c, stage):
        for k in (1, 2, 3):
            gather_copy(buf, which, c, stage, k).wait_recv()

    def scatter_copy(t, c, stage, k):
        first = SCATTER_ORDER[c]
        second = "z" if first == "x" else "x"
        if stage == 0:
            pa, pb = spot(first, k)
            if first == "x":
                src = part.at[t, :, pb, :, cols(c)]
            else:
                src = part.at[t, pa, :, :, cols(c)]
            dst = recv1.at[t, k - 1, :, :, cols(c)]
            axis = first
        else:
            pa, pb = spot(second, k)
            src = mid.at[t, pa if second == "z" else pb, :, cols(c)]
            dst = recv2.at[t, k - 1, :, cols(c)]
            axis = second
        return remote(src, dst, rs_send.at[t, c, stage, k - 1], rs_recv.at[t, c, stage, k - 1], peer(axis, k))

    def scatter_start(t, c, stage):
        for k in (1, 2, 3):
            copy = scatter_copy(t, c, stage, k)
            copy.start()
            sent.append(copy)

    def scatter_wait(t, c, stage):
        for k in (1, 2, 3):
            scatter_copy(t, c, stage, k).wait_recv()

    def scatter_middle(t, c):
        scatter_wait(t, c, 0)
        if SCATTER_ORDER[c] == "x":
            own = part[t, :, b, :, cols(c)]
        else:
            own = part[t, a, :, :, cols(c)]
        total = own.astype(F32)
        for k in range(3):
            total = total + recv1[t, k, :, :, cols(c)].astype(F32)
        mid[t, :, :, cols(c)] = total.astype(BF16)
        scatter_start(t, c, 1)

    def scatter_finish(t, c, incoming):
        scatter_wait(t, c, 1)
        own = mid[t, a if SCATTER_ORDER[c] == "x" else b, :, cols(c)]
        total = own.astype(F32)
        for k in range(3):
            total = total + recv2[t, k, :, cols(c)].astype(F32)
        for blk in range(2):
            base = incoming(blk, c).astype(F32)
            added = base + jnp.where(blocks[t] == blk, total, 0.0)
            passed[0, t, blk, :, cols(c)] = added.astype(BF16)

    def up_chunk(t, c):
        lhs = wout[:, cols(c)]
        rhs = rows[t, :, :, :, cols(c)].reshape(SIDE * SIDE * 8, cols_of)
        term = lax.dot_general(lhs, rhs, (((1,), (1,)), ((), ())), preferred_element_type=F32)
        if c == 0:
            up[...] = term
        else:
            up[...] += term

    def nonlinear(t):
        gate_row = gates[0, pl.ds(slots[t], 1), :]
        pre = pre_t[t]
        active = jnp.maximum(pre, 0.0)
        upstream = up[...]
        grad = jnp.where(pre > 0, upstream * gate_row, 0.0)
        hid_t[:, t * 128 : (t + 1) * 128] = grad.astype(BF16)
        wgt_t[:, t * 128 : (t + 1) * 128] = (active * gate_row).astype(BF16)
        gpart[t : t + 1, :] = jnp.sum(active * upstream, axis=0, keepdims=True)
        hid[...] = grad.T.astype(BF16)

    def part_chunk(t, c):
        term = jnp.dot(hid[...], win[:, cols(c)], preferred_element_type=F32)
        part[t, :, :, :, cols(c)] = term.reshape(SIDE, SIDE, 8, cols_of).astype(BF16)
        scatter_start(t, c, 0)

    def permute_copy(c):
        return remote(
            passed.at[0, 0, :, :, cols(c)], inc.at[:, :, cols(c)], pm_send.at[c], pm_recv.at[c], (below, d)
        )

    every = range(CHUNKS)
    for c in every:
        gather_start(rows.at[0], 0, c, 0)
    for t in range(ticks):
        pre_t[t] = hidden[0, slots[t]].astype(F32).T
    for c in every:
        gather_wait(rows.at[0], 0, c, 0)
        gather_start(rows.at[0], 0, c, 1)
    for c in every:
        gather_start(saved.at[0], 2, c, 0)
    load_out.wait()
    for c in every:
        gather_wait(rows.at[0], 0, c, 1)
        up_chunk(0, c)
    nonlinear(0)
    load_in.wait()
    for c in every:
        part_chunk(0, c)
    for c in every:
        gather_wait(saved.at[0], 2, c, 0)
        gather_start(saved.at[0], 2, c, 1)

    top = s == sections - 1

    def relay_in(c):
        permute_copy(c).wait_recv()
        for blk in range(2):
            inc[blk, :, cols(c)] = jnp.where(top, loss[0, blk, :, cols(c)], inc[blk, :, cols(c)])
        rows[1, a, b, :, cols(c)] = jnp.where(blocks[1] == 0, inc[0, :, cols(c)], inc[1, :, cols(c)])
        gather_start(rows.at[1], 1, c, 0)

    def finish0(c):
        scatter_finish(0, c, lambda blk, c: arriving[0, blk, :, cols(c)])
        copy = permute_copy(c)
        copy.start()
        sent.append(copy)

    def forward1(c):
        gather_wait(rows.at[1], 1, c, 0)
        gather_start(rows.at[1], 1, c, 1)

    def use1(c):
        gather_wait(rows.at[1], 1, c, 1)
        up_chunk(1, c)

    steps = (functools.partial(scatter_middle, 0), finish0, relay_in, forward1, use1)
    for time in range(CHUNKS + len(steps) - 1):
        for j, step in enumerate(steps):
            if 0 <= time - j < CHUNKS:
                step(time - j)
        if time == CHUNKS - 1:
            for c in every:
                gather_start(saved.at[1], 3, c, 0)
    nonlinear(1)
    for c in every:
        part_chunk(1, c)
    for c in every:
        gather_wait(saved.at[1], 3, c, 0)
        gather_start(saved.at[1], 3, c, 1)

    gate_z[a] = gpart[...]
    for k in (1, 2, 3):
        copy = remote(gate_z.at[a], gate_z.at[a], gt_send.at[0, k - 1], gt_recv.at[0, k - 1], peer("z", k))
        copy.start()
        sent.append(copy)

    for c in every:
        scatter_middle(1, c)

    for k in (1, 2, 3):
        remote(gate_z.at[a], gate_z.at[a], gt_send.at[0, k - 1], gt_recv.at[0, k - 1], peer("z", k)).wait_recv()
    gate_x[b] = (gate_z[0] + gate_z[1]) + (gate_z[2] + gate_z[3])
    for k in (1, 2, 3):
        copy = remote(gate_x.at[b], gate_x.at[b], gt_send.at[1, k - 1], gt_recv.at[1, k - 1], peer("x", k))
        copy.start()
        sent.append(copy)

    tile = 512
    flushes = []

    def grad_tiles(weights, buf, staged, out, lane):
        def body(i, _):
            where = pl.ds(pl.multiple_of(i * tile, tile), tile)
            low = buf[0, :, :, :, where].reshape(SIDE * SIDE * 8, tile)
            high = buf[1, :, :, :, where].reshape(SIDE * SIDE * 8, tile)
            total = jnp.dot(weights[:, :128], low, preferred_element_type=F32)
            total += jnp.dot(weights[:, 128:], high, preferred_element_type=F32)
            staged[:, where] = total.astype(BF16)
            return 0

        lax.fori_loop(0, width // tile, body, 0)
        copy = pltpu.make_async_copy(staged, out.at[0], local.at[lane])
        copy.start()
        flushes.append(copy)

    grad_tiles(wgt_t, rows, out_out, grad_out, 2)
    for t in range(ticks):
        for c in every:
            if t == 0:
                gather_wait(saved.at[0], 2, c, 1)
            else:
                gather_wait(saved.at[1], 3, c, 1)
    grad_tiles(hid_t, saved, out_in, grad_in, 3)

    for c in every:
        scatter_finish(1, c, lambda blk, c: inc[blk, :, cols(c)])

    for k in (1, 2, 3):
        remote(gate_x.at[b], gate_x.at[b], gt_send.at[1, k - 1], gt_recv.at[1, k - 1], peer("x", k)).wait_recv()
    sums = (gate_x[0] + gate_x[1]) + (gate_x[2] + gate_x[3])
    for r in range(ticks):
        gate_grads[0, r : r + 1, :] = jnp.where(slots[0] == r, sums[0:1], sums[1:2])

    for copy in sent:
        copy.wait_send()
    for copy in flushes:
        copy.wait()


def per_device(w_in, w_out, stash, hidden, gates, pick, order, arriving, loss):
    _, fw, width = w_in.shape
    ticks = order.shape[1]
    vmem = pl.BlockSpec(memory_space=pltpu.VMEM)
    smem = pl.BlockSpec(memory_space=pltpu.SMEM)
    hbm = pl.BlockSpec(memory_space=pl.ANY)
    dma = pltpu.SemaphoreType.DMA
    return pl.pallas_call(
        kernel,
        name="window",
        out_shape=(
            jax.ShapeDtypeStruct((1, ticks, 2, 8, width), BF16),
            jax.ShapeDtypeStruct((1, fw, width), BF16),
            jax.ShapeDtypeStruct((1, fw, width), BF16),
            jax.ShapeDtypeStruct((1, ticks, 128), F32),
        ),
        in_specs=[hbm, hbm, vmem, vmem, vmem, smem, smem, vmem, vmem],
        out_specs=(vmem, hbm, hbm, vmem),
        scratch_shapes=[
            pltpu.VMEM((fw, width), BF16),
            pltpu.VMEM((fw, width), BF16),
            pltpu.VMEM((ticks, SIDE, SIDE, 8, width), BF16),
            pltpu.VMEM((ticks, SIDE, SIDE, 8, width), BF16),
            pltpu.VMEM((ticks, SIDE, SIDE, 8, width), BF16),
            pltpu.VMEM((ticks, 3, SIDE, 8, width), BF16),
            pltpu.VMEM((ticks, SIDE, 8, width), BF16),
            pltpu.VMEM((ticks, 3, 8, width), BF16),
            pltpu.VMEM((2, 8, width), BF16),
            pltpu.VMEM((fw, 128), F32),
            pltpu.VMEM((fw, ticks * 128), BF16),
            pltpu.VMEM((fw, ticks * 128), BF16),
            pltpu.VMEM((128, fw), BF16),
            pltpu.VMEM((ticks, fw, 128), F32),
            pltpu.VMEM((8, 128), F32),
            pltpu.VMEM((SIDE, 8, 128), F32),
            pltpu.VMEM((SIDE, 8, 128), F32),
            pltpu.VMEM((fw, width), BF16),
            pltpu.VMEM((fw, width), BF16),
            dma((4, CHUNKS, 2, 3)),
            dma((4, CHUNKS, 2, 3)),
            dma((ticks, CHUNKS, 2, 3)),
            dma((ticks, CHUNKS, 2, 3)),
            dma((CHUNKS,)),
            dma((CHUNKS,)),
            dma((2, 3)),
            dma((2, 3)),
            dma((4,)),
        ],
        compiler_params=pltpu.CompilerParams(
            collective_id=0, has_side_effects=True, vmem_limit_bytes=48 * 2**20
        ),
    )(w_in, w_out, stash, hidden, gates, pick, order, arriving, loss)


def solution(mesh):
    placed = (
        P("section", "dp", None),
        P("section", "dp", None),
        P("section", None, "dp", None),
        P("section", None, None, "dp"),
        P("section", None, None),
        P("section", None),
        P("section", None),
        P("section", None, "dp", None),
        P(None, None, "dp", None),
    )
    return jax.shard_map(
        per_device,
        mesh=mesh,
        in_specs=placed,
        out_specs=(
            P("section", None, None, "dp", None),
            P("section", "dp", None),
            P("section", "dp", None),
            P("section", None, None),
        ),
        check_vma=False,
    )
```

time: 432 us -> 106 us (0.25)
  waiting for transfers between devices: 322 us -> 0 us
  Pallas kernels: 0 us -> 94.4 us
  blocking collectives: 42.8 us -> 0 us
  matrix products: 29.8 us -> 0 us
  between operations: 22 us -> 0.66 us
  other arithmetic: 5.06 us -> 0 us
    reduce_scatter x2 -> x0, waiting for transfers between devices: 170 us -> none  [section_tick(): lax.psum_scatter(jnp.dot(hid_grad, in_weight, preferred_element_type=jnp....]
    all_gather x4 -> x0, waiting for transfers between devices: 151 us -> none  [the longest x2 107 us: section_tick(): lax.all_gather(own_rows, 'dp', axis=0, tiled=True)]
    pallas_call x0 -> x1, Pallas kernels: none -> 94.4 us  [per_device(): pl.pallas_call(kernel, name='window', out_shape=(jax.ShapeDtypeStruct((1,...]
    psum x1 -> x0, blocking collectives: 42.8 us -> none  [section_tick(): gate_part = lax.psum(gate_part, 'dp')]
    dot_general x9 -> x0, matrix products: 29.8 us -> none  [the longest x2 9.57 us: weight_terms(): lax.dot_general(weighted, rows_grad, contract, preferred_element_type=jnp...]
    unnamed x12 -> x17, local copies, waits for them, and re-layouts: 0.03 us -> 10 us
    dynamic_slice x4 -> x0, local copies, waits for them, and re-layouts: 4.98 us -> none  [the longest x2 2.12 us: section_tick(): own_rows = incoming[block_id]]
  transfers between devices with their start and end apart: 7 -> 0, of which waited for: 7 -> 0; matrix products, arithmetic and copies ran while one was open for 7% -> 0% of each run, Pallas kernels for 0% -> 0%
where the time goes in v1:
time: 106 us; the launch traced here: 105 us
  Pallas kernels  94.4 us (89%)
  local copies, waits for them, and re-layouts  10 us (9%)
    pallas_call x1, Pallas kernels, per_device(): pl.pallas_call(kernel, name='window', out_shape=(jax.ShapeDtypeStruct((1,...  94.4 us
    unnamed x17, local copies, waits for them, and re-layouts  10 us

profile of v1, /device:TPU:8, one launch (start us, length us, event | category | flops | bytes accessed | tf_op | source)
XLA Modules:
  0.0 105.1 jit_solution(1114884887638144267)
XLA Ops:
  0.6 1.1 %copy.13.hidden = bf16[1,2,128,320]{3,2,1,0:T(8,128)(2,1)S(1)} copy(bf16[1,2,128,320]{2,3,1,0:T(8,128)(2,1)} %param.12) | data formatting | bytes 327680 | tf_op args[3]
  1.7 0.0 copy-start
  1.7 0.9 copy-done
  2.6 0.0 copy-start.1
  2.6 0.9 copy-done.1
  3.5 0.0 copy-start.2
  3.5 0.9 copy-done.2
  4.4 0.0 copy-start.3
  4.4 0.7 copy-done.3
  5.1 0.0 copy-start.4
  5.1 0.7 copy-done.4
  5.8 0.0 copy-start.5
  5.8 0.7 copy-done.5
  6.4 94.4 %window.1 = (bf16[1,2,2,8,4096]{4,3,2,1,0:T(8,128)(2,1)S(1)}, bf16[1,320,4096]{2,1,0:T(8,128)(2,1)S(1)}, bf16[1,320,4096]{2,1,0:T(8,128)(2,1)S(1)}, f32[1,2,128]{2,1,0:T(2,128)S(1)}) custom-call(bf16[1,320,4096]{2,1,0:T(8,128)(2,1)} %w_in.1, bf16[1,320,4096]{2,1,0:T(8,128)(2,1)} %w_out.1, bf16[1,2,8,4096]{3,2,1,0:T(8,128)(2,1)S(1)} %copy-done, ...), custom_call_target="tpu_custom_call" | custom-call | tf_op jit(solution)/shard_map/window/pallas_call | solution.py:302
  100.8 0.7 copy.18
  101.5 1.5 %copy.19 = bf16[1,320,4096]{2,1,0:T(8,128)(2,1)} copy(bf16[1,320,4096]{2,1,0:T(8,128)(2,1)S(1)} %get-tuple-element.9) | data formatting | bytes 5242880
  103.0 1.5 %copy.20 = bf16[1,320,4096]{2,1,0:T(8,128)(2,1)} copy(bf16[1,320,4096]{2,1,0:T(8,128)(2,1)S(1)} %get-tuple-element.10) | data formatting | bytes 5242880
  104.5 0.6 copy.21
Async XLA Ops:
  1.7 0.9 copy-start
  2.6 0.9 copy-start.1
  3.5 0.9 copy-start.2
  4.4 0.7 copy-start.3
  5.1 0.7 copy-start.4
  5.8 0.7 copy-start.5

commit v2 on v1

v2 whole, which is shorter than its diff:
```python
import functools

import jax
import jax.numpy as jnp
from jax import lax
from jax.experimental import pallas as pl
from jax.experimental.pallas import tpu as pltpu
from jax.sharding import PartitionSpec as P

MESH = pl.DeviceIdType.MESH
SIDE = 4
FIRST = ("z", "x")
STARTS = (0, 2688)
SIZES = (2688, 1408)
CHUNKS = len(FIRST)
LATER = (1, 0)
BF16 = jnp.bfloat16
F32 = jnp.float32


def kernel(
    w_in, w_out, stash_hbm, hidden_hbm, gates_hbm, pick_hbm, order_hbm, arriving_hbm, loss_hbm,
    passed, grad_in, grad_out, gate_grads,
    stash, hidden, gates, pick, order, arriving, loss,
    win, wout, rows, saved, part, relay, recv1, mid, recv2, base, back, inc, mask_out, mask_in, up, hid_t, wgt_t, hid, gpart, gate_z, gate_x,
    ag_send, ag_recv, rs_send, rs_recv, pm_send, pm_recv, gt_send, gt_recv, local,
):
    ticks, width = 2, w_in.shape[2]
    s, d = lax.axis_index("section"), lax.axis_index("dp")
    a, b = d // SIDE, d % SIDE
    sections = lax.axis_size("section")
    below, above = lax.rem(s + sections - 1, sections), lax.rem(s + 1, sections)

    def spot(axis, k):
        return ((a + k) % SIDE if axis == "z" else a, (b + k) % SIDE if axis == "x" else b)

    def peer(axis, k):
        pa, pb = spot(axis, k)
        return (s, pa * SIDE + pb)

    def cols(c):
        return pl.ds(STARTS[c], SIZES[c])

    barrier = pltpu.get_barrier_semaphore()
    for axis in ("z", "x"):
        for k in (1, 2, 3):
            pl.semaphore_signal(barrier, inc=1, device_id=peer(axis, k), device_id_type=MESH)
    for k in range(SIDE):
        for axis in ("z", "x"):
            if k or axis == "z":
                pa, pb = spot(axis, k)
                for section in (below, above):
                    there = (section, pa * SIDE + pb)
                    pl.semaphore_signal(barrier, inc=1, device_id=there, device_id_type=MESH)

    pairs = (
        (order_hbm, order), (pick_hbm, pick), (arriving_hbm, arriving), (stash_hbm, stash), (w_out.at[0], wout),
        (hidden_hbm, hidden), (gates_hbm, gates), (w_in.at[0], win), (loss_hbm, loss),
    )
    loads = [pltpu.make_async_copy(src, dst, local.at[i]) for i, (src, dst) in enumerate(pairs)]
    for load in loads:
        load.start()
    waiting = list(loads)

    def loaded(count):
        for _ in range(count):
            waiting.pop(0).wait()

    loaded(4)

    slots = [order[0, t] for t in range(ticks)]
    blocks = [pick[0, slots[t]] for t in range(ticks)]
    rows[0, a, b] = arriving[0, blocks[0]]
    for t in range(ticks):
        saved[t, a, b] = stash[0, slots[t]]

    mask_out[...] = jnp.zeros(mask_out.shape, F32) + blocks[0].astype(F32)
    top = s == sections - 1
    pl.semaphore_wait(barrier, 6 + 2 * 7)

    gpart[...] = jnp.zeros_like(gpart)
    sent = []
    pending = {}

    def remote(src, dst, send_sem, recv_sem, device):
        return pltpu.make_async_remote_copy(
            src_ref=src, dst_ref=dst, send_sem=send_sem, recv_sem=recv_sem, device_id=device, device_id_type=MESH
        )

    def launch(key, copy):
        copy.start()
        sent.append(copy)
        pending[key] = copy

    def arrive(*key):
        pending.pop(key).wait_recv()

    def finish():
        loaded(len(waiting))
        for copy in pending.values():
            copy.wait_recv()
        for copy in sent:
            copy.wait_send()

    def other(axis):
        return "x" if axis == "z" else "z"

    def line(buf, axis, k, c, half=slice(None)):
        pa, pb = spot(axis, k)
        return buf.at[half, pb, :, cols(c)] if axis == "x" else buf.at[pa, half, :, cols(c)]

    low, high = pl.ds(0, SIDE // 2), pl.ds(SIDE // 2, SIDE // 2)

    def gather_first(buf, which, c):
        axis = FIRST[c]
        view = buf.at[a, b, :, cols(c)]
        for k in (2, 1, 3):
            sems = ag_send.at[which, c, k - 1], ag_recv.at[which, c, k - 1]
            launch(("g", which, c, k), remote(view, view, *sems, peer(axis, k)))

    def gather_second(buf, which, c):
        for k in (3, 2, 1):
            arrive("g", which, c, k)
        axis = other(FIRST[c])
        for i, (k, half) in enumerate(((1, low), (3, high), (1, high), (3, low))):
            view = line(buf, axis, 0, c, half)
            sems = ag_send.at[which, c, 3 + i], ag_recv.at[which, c, 3 + i]
            launch(("h", which, c, i), remote(view, view, *sems, peer(axis, k)))

    def gather_third(buf, which, c):
        axis = other(FIRST[c])
        for i, (k, half) in enumerate(((1, low), (3, high))):
            arrive("h", which, c, i)
            view = line(buf, axis, SIDE - k, c, half)
            sems = ag_send.at[which, c, 7 + i], ag_recv.at[which, c, 7 + i]
            launch(("i", which, c, i), remote(view, view, *sems, peer(axis, k)))

    def gather_end(which, c):
        for i in (2, 3):
            arrive("h", which, c, i)
        for i in (0, 1):
            arrive("i", which, c, i)

    halves = ((1, low, high, 0), (3, high, low, 1))

    def scatter_first(t, c):
        axis = other(FIRST[c])
        for k, half, rest, i in halves:
            src = line(part.at[t], axis, 2, c, half)
            sems = rs_send.at[t, c, i], rs_recv.at[t, c, i]
            launch(("s", t, c, i), remote(src, relay.at[t, i, :, :, cols(c)], *sems, peer(axis, k)))
        for k, half, rest, i in halves:
            src = line(part.at[t], axis, k, c, rest)
            sems = rs_send.at[t, c, 2 + i], rs_recv.at[t, c, 2 + i]
            launch(("w", t, c, i), remote(src, recv1.at[t, i, rest, :, cols(c)], *sems, peer(axis, k)))

    def scatter_second(t, c):
        axis = other(FIRST[c])
        for k, half, rest, i in halves:
            arrive("s", t, c, i)
            pa, pb = spot(axis, k)
            where = (t, half, pb, slice(None), cols(c)) if axis == "x" else (t, pa, half, slice(None), cols(c))
            part[where] = (part[where].astype(F32) + relay[t, i, :, :, cols(c)].astype(F32)).astype(BF16)
            src = line(part.at[t], axis, k, c, half)
            sems = rs_send.at[t, c, 4 + i], rs_recv.at[t, c, 4 + i]
            launch(("u", t, c, i), remote(src, recv1.at[t, i, half, :, cols(c)], *sems, peer(axis, k)))

    def scatter_third(t, c):
        axis = other(FIRST[c])
        own = part[t, :, b, :, cols(c)] if axis == "x" else part[t, a, :, :, cols(c)]
        total = own.astype(F32)
        for i in (0, 1):
            arrive("w", t, c, i)
            arrive("u", t, c, i)
            total = total + recv1[t, i, :, :, cols(c)].astype(F32)
        mid[t, :, :, cols(c)] = total.astype(BF16)
        axis = FIRST[c]
        for k in (2, 1, 3, 0) if t == 0 else (2, 1, 3):
            pa, pb = spot(axis, k)
            src = mid.at[t, pa if axis == "z" else pb, :, cols(c)]
            sems = rs_send.at[t, c, 6 + k], rs_recv.at[t, c, 6 + k]
            there = (below if t == 0 else s, pa * SIDE + pb)
            launch(("v", t, c, k), remote(src, recv2.at[t, k, :, cols(c)], *sems, there))

    def relay_in(c):
        total = None
        for k in (0, 3, 1, 2):
            arrive("v", 0, c, k)
            term = recv2[0, k, :, cols(c)].astype(F32)
            total = term if total is None else total + term
        if c == LATER[0]:
            arrive("b", 0)
            arrive("b", 1)
        choice = mask_in[:, 0:1]
        for blk in range(2):
            added = base[blk, :, cols(c)].astype(F32) + jnp.where(choice == blk, total, 0.0)
            back[blk, :, cols(c)] = added.astype(BF16)
            inc[blk, :, cols(c)] = jnp.where(top, loss[0, blk, :, cols(c)], back[blk, :, cols(c)])
        rows[1, a, b, :, cols(c)] = jnp.where(blocks[1] == 0, inc[0, :, cols(c)], inc[1, :, cols(c)])
        gather_first(rows.at[1], 1, c)

    def give_back(c):
        src = back.at[:, :, cols(c)]
        dst = passed.at[0, 0, :, :, cols(c)]
        launch(("r", c), remote(src, dst, pm_send.at[c], pm_recv.at[c], (above, d)))

    def base_out():
        src = arriving.at[0]
        launch(("b", 0), remote(src, base, pm_send.at[CHUNKS], pm_recv.at[CHUNKS], (below, d)))
        last = CHUNKS + 1
        launch(("b", 1), remote(mask_out, mask_in, pm_send.at[last], pm_recv.at[last], (below, d)))

    def scatter_finish(c):
        total = mid[1, a if FIRST[c] == "z" else b, :, cols(c)].astype(F32)
        for k in (1, 3, 2):
            arrive("v", 1, c, k)
            total = total + recv2[1, k, :, cols(c)].astype(F32)
        for blk in range(2):
            added = inc[blk, :, cols(c)].astype(F32) + jnp.where(blocks[1] == blk, total, 0.0)
            passed[0, 1, blk, :, cols(c)] = added.astype(BF16)

    def up_chunk(t, c, fresh):
        lhs = wout[:, cols(c)]
        rhs = rows[t, :, :, :, cols(c)].reshape(SIDE * SIDE * 8, SIZES[c])
        term = lax.dot_general(lhs, rhs, (((1,), (1,)), ((), ())), preferred_element_type=F32)
        if fresh:
            up[...] = term
        else:
            up[...] += term

    def nonlinear(t):
        gate_row = gates[0, pl.ds(slots[t], 1), :]
        pre = hidden[0, slots[t]].astype(F32)
        active = jnp.maximum(pre, 0.0)
        upstream = up[...]
        grad = jnp.where(pre > 0, upstream * gate_row, 0.0)
        hid_t[:, t * 128 : (t + 1) * 128] = grad.astype(BF16)
        wgt_t[:, t * 128 : (t + 1) * 128] = (active * gate_row).astype(BF16)
        gpart[t : t + 1, :] = jnp.sum(active * upstream, axis=0, keepdims=True)
        hid[...] = grad.T.astype(BF16)

    def part_chunk(t, c):
        term = jnp.dot(hid[...], win[:, cols(c)], preferred_element_type=F32)
        part[t, :, :, :, cols(c)] = term.reshape(SIDE, SIDE, 8, SIZES[c]).astype(BF16)
        scatter_first(t, c)

    every = range(CHUNKS)
    for c in every:
        gather_first(rows.at[0], 0, c)
    base_out()
    for c in every:
        gather_second(rows.at[0], 0, c)
    for c in every:
        gather_third(rows.at[0], 0, c)
    for c in every:
        gather_first(saved.at[0], 2, c)
    for c in every:
        gather_first(saved.at[1], 3, c)
    loaded(3)
    for c in every:
        gather_end(0, c)
        up_chunk(0, c, c == 0)
    nonlinear(0)
    loaded(2)
    for c in LATER:
        part_chunk(0, c)
    for c in every:
        gather_second(saved.at[0], 2, c)
    for c in LATER:
        scatter_second(0, c)
    for c in every:
        gather_third(saved.at[0], 2, c)
    for c in LATER:
        scatter_third(0, c)
    for c in every:
        gather_second(saved.at[1], 3, c)
    for c in LATER:
        relay_in(c)
    for c in LATER:
        gather_second(rows.at[1], 1, c)
    for c in LATER:
        give_back(c)
    for c in LATER:
        gather_third(rows.at[1], 1, c)
    for c in every:
        gather_third(saved.at[1], 3, c)
    for c in LATER:
        gather_end(1, c)
        up_chunk(1, c, c == LATER[0])
    nonlinear(1)
    for c in LATER:
        part_chunk(1, c)

    gate_z[a] = gpart[...]
    for k in (1, 2, 3):
        view = gate_z.at[a]
        launch(("t", 0, k), remote(view, view, gt_send.at[0, k - 1], gt_recv.at[0, k - 1], peer("z", k)))

    for c in LATER:
        scatter_second(1, c)
    for c in LATER:
        scatter_third(1, c)

    for k in (1, 2, 3):
        arrive("t", 0, k)
    gate_x[b] = (gate_z[0] + gate_z[1]) + (gate_z[2] + gate_z[3])
    for k in (1, 2, 3):
        view = gate_x.at[b]
        launch(("t", 1, k), remote(view, view, gt_send.at[1, k - 1], gt_recv.at[1, k - 1], peer("x", k)))

    tile = 512

    def grad_tiles(weights, buf, out):
        def body(i, _):
            where = pl.ds(pl.multiple_of(i * tile, tile), tile)
            low = buf[0, :, :, :, where].reshape(SIDE * SIDE * 8, tile)
            high = buf[1, :, :, :, where].reshape(SIDE * SIDE * 8, tile)
            total = jnp.dot(weights[:, :128], low, preferred_element_type=F32)
            total += jnp.dot(weights[:, 128:], high, preferred_element_type=F32)
            out[0, :, where] = total.astype(BF16)
            return 0

        lax.fori_loop(0, width // tile, body, 0)

    grad_tiles(wgt_t, rows, grad_out)
    for t in range(ticks):
        for c in every:
            gather_end(2 + t, c)
    grad_tiles(hid_t, saved, grad_in)

    for c in LATER:
        scatter_finish(c)
    for c in every:
        arrive("r", c)

    for k in (1, 2, 3):
        arrive("t", 1, k)
    sums = (gate_x[0] + gate_x[1]) + (gate_x[2] + gate_x[3])
    for r in range(ticks):
        gate_grads[0, r : r + 1, :] = jnp.where(slots[0] == r, sums[0:1], sums[1:2])

    finish()


def flush(*refs):
    sems = refs[8]
    copies = [pltpu.make_async_copy(refs[i], refs[4 + i], sems.at[i]) for i in (1, 2, 0, 3)]
    for copy in copies:
        copy.start()
    for copy in copies:
        copy.wait()


def per_device(w_in, w_out, stash, hidden, gates, pick, order, arriving, loss):
    _, fw, width = w_in.shape
    ticks = order.shape[1]
    vmem = pl.BlockSpec(memory_space=pltpu.VMEM)
    hbm = pl.BlockSpec(memory_space=pltpu.HBM)
    hidden = jnp.swapaxes(hidden, 2, 3)
    dma = pltpu.SemaphoreType.DMA
    operands = (w_in, w_out, stash, hidden, gates, pick, order, arriving, loss)
    results = pl.pallas_call(
        kernel,
        name="window",
        out_shape=(
            jax.ShapeDtypeStruct((1, ticks, 2, 8, width), BF16),
            jax.ShapeDtypeStruct((1, fw, width), BF16),
            jax.ShapeDtypeStruct((1, fw, width), BF16),
            jax.ShapeDtypeStruct((1, ticks, 128), F32),
        ),
        in_specs=[hbm] * 9,
        out_specs=(vmem, vmem, vmem, vmem),
        scratch_shapes=[
            pltpu.VMEM(stash.shape, BF16),
            pltpu.VMEM(hidden.shape, BF16),
            pltpu.VMEM(gates.shape, F32),
            pltpu.SMEM(pick.shape, jnp.int32),
            pltpu.SMEM(order.shape, jnp.int32),
            pltpu.VMEM(arriving.shape, BF16),
            pltpu.VMEM(loss.shape, BF16),
            pltpu.VMEM((fw, width), BF16),
            pltpu.VMEM((fw, width), BF16),
            pltpu.VMEM((ticks, SIDE, SIDE, 8, width), BF16),
            pltpu.VMEM((ticks, SIDE, SIDE, 8, width), BF16),
            pltpu.VMEM((ticks, SIDE, SIDE, 8, width), BF16),
            pltpu.VMEM((ticks, 2, SIDE // 2, 8, width), BF16),
            pltpu.VMEM((ticks, 2, SIDE, 8, width), BF16),
            pltpu.VMEM((ticks, SIDE, 8, width), BF16),
            pltpu.VMEM((ticks, SIDE, 8, width), BF16),
            pltpu.VMEM((2, 8, width), BF16),
            pltpu.VMEM((2, 8, width), BF16),
            pltpu.VMEM((2, 8, width), BF16),
            pltpu.VMEM((8, 128), F32),
            pltpu.VMEM((8, 128), F32),
            pltpu.VMEM((fw, 128), F32),
            pltpu.VMEM((fw, ticks * 128), BF16),
            pltpu.VMEM((fw, ticks * 128), BF16),
            pltpu.VMEM((128, fw), BF16),
            pltpu.VMEM((8, 128), F32),
            pltpu.VMEM((SIDE, 8, 128), F32),
            pltpu.VMEM((SIDE, 8, 128), F32),
            dma((4, CHUNKS, 9)),
            dma((4, CHUNKS, 9)),
            dma((ticks, CHUNKS, 10)),
            dma((ticks, CHUNKS, 10)),
            dma((CHUNKS + 2,)),
            dma((CHUNKS + 2,)),
            dma((2, 3)),
            dma((2, 3)),
            dma((9,)),
        ],
        compiler_params=pltpu.CompilerParams(
            collective_id=0, has_side_effects=True, vmem_limit_bytes=40 * 2**20
        ),
    )(*[pltpu.with_memory_space_constraint(x, pltpu.HBM) for x in operands])
    return pl.pallas_call(
        flush,
        name="flush",
        out_shape=[jax.ShapeDtypeStruct(x.shape, x.dtype) for x in results],
        in_specs=[pl.BlockSpec(memory_space=pl.ANY)] * 4,
        out_specs=[hbm] * 4,
        scratch_shapes=[dma((4,))],
        compiler_params=pltpu.CompilerParams(vmem_limit_bytes=2**20),
    )(*results)


def solution(mesh):
    placed = (
        P("section", "dp", None),
        P("section", "dp", None),
        P("section", None, "dp", None),
        P("section", None, None, "dp"),
        P("section", None, None),
        P("section", None),
        P("section", None),
        P("section", None, "dp", None),
        P(None, None, "dp", None),
    )
    return jax.shard_map(
        per_device,
        mesh=mesh,
        in_specs=placed,
        out_specs=(
            P("section", None, None, "dp", None),
            P("section", "dp", None),
            P("section", "dp", None),
            P("section", None, None),
        ),
        check_vma=False,
    )
```

time: 106 us -> 89.6 us (0.85)
  local copies, waits for them, and re-layouts: 10 us -> 0 us
  Pallas kernels: 94.4 us -> 87.9 us
    unnamed x17 -> x0, local copies, waits for them, and re-layouts: 10 us -> none
    pallas_call x1, Pallas kernels: 94.4 us -> 85.5 us  [per_device(): pl.pallas_call(kernel, name='window', out_shape=(jax.ShapeDtypeStruct((1,...]
    pallas_call x0 -> x1, Pallas kernels: none -> 2.47 us  [per_device(): pl.pallas_call(flush, name='flush', out_shape=[jax.ShapeDtypeStruct(x.sha...]
where the time goes in v2:
time: 89.6 us; the launch traced here: 88.6 us
  Pallas kernels  87.9 us (98%)
    pallas_call x1, Pallas kernels, per_device(): pl.pallas_call(kernel, name='window', out_shape=(jax.ShapeDtypeStruct((1,...  85.5 us
    pallas_call x1, Pallas kernels, per_device(): pl.pallas_call(flush, name='flush', out_shape=[jax.ShapeDtypeStruct(x.sha...  2.47 us

profile of v2, /device:TPU:8, one launch (start us, length us, event | category | flops | bytes accessed | tf_op | source)
XLA Modules:
  0.0 88.6 jit_solution(18162444972557998695)
XLA Ops:
  0.6 85.5 %window.1 = (bf16[1,2,2,8,4096]{4,3,2,1,0:T(8,128)(2,1)S(1)}, bf16[1,320,4096]{2,1,0:T(8,128)(2,1)S(1)}, bf16[1,320,4096]{2,1,0:T(8,128)(2,1)S(1)}, f32[1,2,128]{2,1,0:T(2,128)S(1)}) custom-call(bf16[1,320,4096]{2,1,0:T(8,128)(2,1)} %w_in.1, bf16[1,320,4096]{2,1,0:T(8,128)(2,1)} %w_out.1, bf16[1,2,8,4096]{3,2,1,0:T(8,128)(2,1)} %stash_hbm.1, ...), custom_call_target="tpu_custom_call" | custom-call | tf_op jit(solution)/shard_map/window/pallas_call | solution.py:362
  86.1 2.5 %flush.1 = (bf16[1,2,2,8,4096]{4,3,2,1,0:T(8,128)(2,1)}, bf16[1,320,4096]{2,1,0:T(8,128)(2,1)}, bf16[1,320,4096]{2,1,0:T(8,128)(2,1)}, f32[1,2,128]{2,1,0:T(2,128)}) custom-call(bf16[1,2,2,8,4096]{4,3,2,1,0:T(8,128)(2,1)S(1)} %get-tuple-element.8.refs_0_, bf16[1,320,4096]{2,1,0:T(8,128)(2,1)S(1)} %get-tuple-element.9.refs_1_, ...), custom_call_target="tpu_custom_call" | custom-call | tf_op jit(solution)/shard_map/flush/pallas_call | solution.py:416

commit v3 on v2

--- a/solution.py
+++ b/solution.py
@@ -9,11 +9,14 @@
 
 MESH = pl.DeviceIdType.MESH
 SIDE = 4
-FIRST = ("z", "x")
-STARTS = (0, 2688)
-SIZES = (2688, 1408)
+FIRST = ('z', 'x', 'z')
+STARTS = (0, 1408, 2816)
+SIZES = (1408, 1408, 1280)
 CHUNKS = len(FIRST)
-LATER = (1, 0)
+LATER = (1, 0, 2)
+SAVED_FIRST = ("z", "z")
+SAVED_STARTS = (0, 2048)
+SAVED_SIZES = (2048, 2048)
 BF16 = jnp.bfloat16
 F32 = jnp.float32
 
@@ -111,27 +114,43 @@
 
     low, high = pl.ds(0, SIDE // 2), pl.ds(SIDE // 2, SIDE // 2)
 
-    def gather_first(buf, which, c):
-        axis = FIRST[c]
-        view = buf.at[a, b, :, cols(c)]
+    def table(which, c):
+        if which == 2:
+            return SAVED_FIRST[c], pl.ds(SAVED_STARTS[c], SAVED_SIZES[c])
+        return FIRST[c], cols(c)
+
+    def pack(which, axis, k, half, columns):
+        pa, pb = spot(axis, k)
+        buf, lead = (saved, slice(None)) if which == 2 else (rows, which)
+        if half is None:
+            return buf.at[lead, pa, pb, :, columns]
+        if axis == "x":
+            return buf.at[lead, half, pb, :, columns]
+        return buf.at[lead, pa, half, :, columns]
+
+    def gather_first(which, c):
+        axis, columns = table(which, c)
+        view = pack(which, axis, 0, None, columns)
         for k in (2, 1, 3):
             sems = ag_send.at[which, c, k - 1], ag_recv.at[which, c, k - 1]
             launch(("g", which, c, k), remote(view, view, *sems, peer(axis, k)))
 
-    def gather_second(buf, which, c):
+    def gather_second(which, c):
         for k in (3, 2, 1):
             arrive("g", which, c, k)
-        axis = other(FIRST[c])
+        axis, columns = table(which, c)
+        axis = other(axis)
         for i, (k, half) in enumerate(((1, low), (3, high), (1, high), (3, low))):
-            view = line(buf, axis, 0, c, half)
+            view = pack(which, axis, 0, half, columns)
             sems = ag_send.at[which, c, 3 + i], ag_recv.at[which, c, 3 + i]
             launch(("h", which, c, i), remote(view, view, *sems, peer(axis, k)))
 
-    def gather_third(buf, which, c):
-        axis = other(FIRST[c])
+    def gather_third(which, c):
+        axis, columns = table(which, c)
+        axis = other(axis)
         for i, (k, half) in enumerate(((1, low), (3, high))):
             arrive("h", which, c, i)
-            view = line(buf, axis, SIDE - k, c, half)
+            view = pack(which, axis, SIDE - k, half, columns)
             sems = ag_send.at[which, c, 7 + i], ag_recv.at[which, c, 7 + i]
             launch(("i", which, c, i), remote(view, view, *sems, peer(axis, k)))
 
@@ -197,7 +216,7 @@
             back[blk, :, cols(c)] = added.astype(BF16)
             inc[blk, :, cols(c)] = jnp.where(top, loss[0, blk, :, cols(c)], back[blk, :, cols(c)])
         rows[1, a, b, :, cols(c)] = jnp.where(blocks[1] == 0, inc[0, :, cols(c)], inc[1, :, cols(c)])
-        gather_first(rows.at[1], 1, c)
+        gather_first(1, c)
 
     def give_back(c):
         src = back.at[:, :, cols(c)]
@@ -246,16 +265,14 @@
 
     every = range(CHUNKS)
     for c in every:
-        gather_first(rows.at[0], 0, c)
+        gather_first(0, c)
     base_out()
     for c in every:
-        gather_second(rows.at[0], 0, c)
+        gather_second(0, c)
     for c in every:
-        gather_third(rows.at[0], 0, c)
-    for c in every:
-        gather_first(saved.at[0], 2, c)
-    for c in every:
-        gather_first(saved.at[1], 3, c)
+        gather_third(0, c)
+    gather_first(2, 0)
+    gather_first(2, 1)
     loaded(3)
     for c in every:
         gather_end(0, c)
@@ -264,26 +281,22 @@
     loaded(2)
     for c in LATER:
         part_chunk(0, c)
-    for c in every:
-        gather_second(saved.at[0], 2, c)
+    gather_second(2, 0)
     for c in LATER:
         scatter_second(0, c)
-    for c in every:
-        gather_third(saved.at[0], 2, c)
     for c in LATER:
         scatter_third(0, c)
-    for c in every:
-        gather_second(saved.at[1], 3, c)
+    gather_second(2, 1)
     for c in LATER:
         relay_in(c)
-    for c in LATER:
-        gather_second(rows.at[1], 1, c)
+    gather_third(2, 0)
+    for c in LATER:
+        gather_second(1, c)
     for c in LATER:
         give_back(c)
     for c in LATER:
-        gather_third(rows.at[1], 1, c)
-    for c in every:
-        gather_third(saved.at[1], 3, c)
+        gather_third(1, c)
+    gather_third(2, 1)
     for c in LATER:
         gather_end(1, c)
         up_chunk(1, c, c == LATER[0])
@@ -323,9 +336,8 @@
         lax.fori_loop(0, width // tile, body, 0)
 
     grad_tiles(wgt_t, rows, grad_out)
-    for t in range(ticks):
-        for c in every:
-            gather_end(2 + t, c)
+    for c in range(len(SAVED_FIRST)):
+        gather_end(2, c)
     grad_tiles(hid_t, saved, grad_in)
 
     for c in LATER:
@@ -399,8 +411,8 @@
             pltpu.VMEM((8, 128), F32),
             pltpu.VMEM((SIDE, 8, 128), F32),
             pltpu.VMEM((SIDE, 8, 128), F32),
-            dma((4, CHUNKS, 9)),
-            dma((4, CHUNKS, 9)),
+            dma((3, max(CHUNKS, len(SAVED_FIRST)), 9)),
+            dma((3, max(CHUNKS, len(SAVED_FIRST)), 9)),
             dma((ticks, CHUNKS, 10)),
             dma((ticks, CHUNKS, 10)),
             dma((CHUNKS + 2,)),

time: 89.6 us -> 85.4 us (0.953); the launches traced: 88.6 us -> 85.3 us
  Pallas kernels: 87.9 us -> 84.7 us
    pallas_call x1, Pallas kernels: 85.5 us -> 82.2 us  [per_device(): pl.pallas_call(kernel, name='window', out_shape=(jax.ShapeDtypeStruct((1,...]
where the time goes in v3:
time: 85.4 us; the launch traced here: 85.3 us
  Pallas kernels  84.7 us (99%)
    pallas_call x1, Pallas kernels, per_device(): pl.pallas_call(kernel, name='window', out_shape=(jax.ShapeDtypeStruct((1,...  82.2 us
    pallas_call x1, Pallas kernels, per_device(): pl.pallas_call(flush, name='flush', out_shape=[jax.ShapeDtypeStruct(x.sha...  2.47 us

profile of v3, /device:TPU:8, one launch (start us, length us, event | category | flops | bytes accessed | tf_op | source)
XLA Modules:
  0.0 85.3 jit_solution(5641436292740684823)
XLA Ops:
  0.6 82.2 %window.1 = (bf16[1,2,2,8,4096]{4,3,2,1,0:T(8,128)(2,1)S(1)}, bf16[1,320,4096]{2,1,0:T(8,128)(2,1)S(1)}, bf16[1,320,4096]{2,1,0:T(8,128)(2,1)S(1)}, f32[1,2,128]{2,1,0:T(2,128)S(1)}) custom-call(bf16[1,320,4096]{2,1,0:T(8,128)(2,1)} %w_in.1, bf16[1,320,4096]{2,1,0:T(8,128)(2,1)} %w_out.1, bf16[1,2,8,4096]{3,2,1,0:T(8,128)(2,1)} %stash_hbm.1, ...), custom_call_target="tpu_custom_call" | custom-call | tf_op jit(solution)/shard_map/window/pallas_call | solution.py:374
  82.9 2.5 %flush.1 = (bf16[1,2,2,8,4096]{4,3,2,1,0:T(8,128)(2,1)}, bf16[1,320,4096]{2,1,0:T(8,128)(2,1)}, bf16[1,320,4096]{2,1,0:T(8,128)(2,1)}, f32[1,2,128]{2,1,0:T(2,128)}) custom-call(bf16[1,2,2,8,4096]{4,3,2,1,0:T(8,128)(2,1)S(1)} %get-tuple-element.8.refs_0_, bf16[1,320,4096]{2,1,0:T(8,128)(2,1)S(1)} %get-tuple-element.9.refs_1_, ...), custom_call_target="tpu_custom_call" | custom-call | tf_op jit(solution)/shard_map/flush/pallas_call | solution.py:428

commit v4 on v3

--- a/solution.py
+++ b/solution.py
@@ -303,24 +303,6 @@
     nonlinear(1)
     for c in LATER:
         part_chunk(1, c)
-
-    gate_z[a] = gpart[...]
-    for k in (1, 2, 3):
-        view = gate_z.at[a]
-        launch(("t", 0, k), remote(view, view, gt_send.at[0, k - 1], gt_recv.at[0, k - 1], peer("z", k)))
-
-    for c in LATER:
-        scatter_second(1, c)
-    for c in LATER:
-        scatter_third(1, c)
-
-    for k in (1, 2, 3):
-        arrive("t", 0, k)
-    gate_x[b] = (gate_z[0] + gate_z[1]) + (gate_z[2] + gate_z[3])
-    for k in (1, 2, 3):
-        view = gate_x.at[b]
-        launch(("t", 1, k), remote(view, view, gt_send.at[1, k - 1], gt_recv.at[1, k - 1], peer("x", k)))
-
     tile = 512
 
     def grad_tiles(weights, buf, out):
@@ -336,6 +318,24 @@
         lax.fori_loop(0, width // tile, body, 0)
 
     grad_tiles(wgt_t, rows, grad_out)
+
+    gate_z[a] = gpart[...]
+    for k in (1, 2, 3):
+        view = gate_z.at[a]
+        launch(("t", 0, k), remote(view, view, gt_send.at[0, k - 1], gt_recv.at[0, k - 1], peer("z", k)))
+
+    for c in LATER:
+        scatter_second(1, c)
+    for c in LATER:
+        scatter_third(1, c)
+
+    for k in (1, 2, 3):
+        arrive("t", 0, k)
+    gate_x[b] = (gate_z[0] + gate_z[1]) + (gate_z[2] + gate_z[3])
+    for k in (1, 2, 3):
+        view = gate_x.at[b]
+        launch(("t", 1, k), remote(view, view, gt_send.at[1, k - 1], gt_recv.at[1, k - 1], peer("x", k)))
+
     for c in range(len(SAVED_FIRST)):
         gather_end(2, c)
     grad_tiles(hid_t, saved, grad_in)

time: 85.4 us -> 84.9 us (level)
  no operation moved by 1% of the time
where the time goes in v4:
time: 84.9 us; the launch traced here: 84.8 us
  Pallas kernels  84.2 us (99%)
    pallas_call x1, Pallas kernels, per_device(): pl.pallas_call(kernel, name='window', out_shape=(jax.ShapeDtypeStruct((1,...  81.7 us
    pallas_call x1, Pallas kernels, per_device(): pl.pallas_call(flush, name='flush', out_shape=[jax.ShapeDtypeStruct(x.sha...  2.47 us

profile of v4, /device:TPU:8, one launch (start us, length us, event | category | flops | bytes accessed | tf_op | source)
XLA Modules:
  0.0 84.8 jit_solution(2618802154915724423)
XLA Ops:
  0.6 81.7 %window.1 = (bf16[1,2,2,8,4096]{4,3,2,1,0:T(8,128)(2,1)S(1)}, bf16[1,320,4096]{2,1,0:T(8,128)(2,1)S(1)}, bf16[1,320,4096]{2,1,0:T(8,128)(2,1)S(1)}, f32[1,2,128]{2,1,0:T(2,128)S(1)}) custom-call(bf16[1,320,4096]{2,1,0:T(8,128)(2,1)} %w_in.1, bf16[1,320,4096]{2,1,0:T(8,128)(2,1)} %w_out.1, bf16[1,2,8,4096]{3,2,1,0:T(8,128)(2,1)} %stash_hbm.1, ...), custom_call_target="tpu_custom_call" | custom-call | tf_op jit(solution)/shard_map/window/pallas_call | solution.py:374
  82.4 2.5 %flush.1 = (bf16[1,2,2,8,4096]{4,3,2,1,0:T(8,128)(2,1)}, bf16[1,320,4096]{2,1,0:T(8,128)(2,1)}, bf16[1,320,4096]{2,1,0:T(8,128)(2,1)}, f32[1,2,128]{2,1,0:T(2,128)}) custom-call(bf16[1,2,2,8,4096]{4,3,2,1,0:T(8,128)(2,1)S(1)} %get-tuple-element.8.refs_0_, bf16[1,320,4096]{2,1,0:T(8,128)(2,1)S(1)} %get-tuple-element.9.refs_1_, ...), custom_call_target="tpu_custom_call" | custom-call | tf_op jit(solution)/shard_map/flush/pallas_call | solution.py:428
